TPU v7x, 32 devices: a whole 2x2x4 slice. The times are simulated.
32 devices in a mesh: row: 8 (over y, x, core), col: 4 (over z).
Axes of the slice: x: 2, y: 2, z: 4, core: 2. Of those that a mesh axis runs over, the one named last changes fastest.
Arguments:
- panel_tiles: float32 [16384, 1024], P('row', 'col'), may hold values from -48 to 48
- left_u: bfloat16 [16384, 6144], P('row', 'col'), may hold values from -8 to 8
- earlier_right_factors: bfloat16 [16384, 6144], P('row', 'col'), may hold values from -0.25 to 0.25
- tile_global_index: int32 [16], replicated, may hold values from 0 to 15, as said below
Outputs:
- panel_factor: float32 [16384, 1024], P('row', 'col')
Inputs may be any that keep to these rules, and one draw needn't show every extreme that they name: `tile_global_index`: A permutation; slot pivot, the one numbered 0, holds the diagonal tile.
All inputs are finite; a program needn't handle non-finite values.
Results may differ from a plain program's by a relative error of at most 0.00053.
Values may be sent and summed in bfloat16 or wider, within the bound.
A program may use at most 128 MiB of HBM per device.

v0:
```python
import functools

import jax
import jax.numpy as jnp
from jax import lax
from jax.experimental import pallas as pl
from jax.experimental.pallas import tpu as pltpu
from jax.sharding import PartitionSpec as P

TILE = 1024
RANK = 256

BLK = 128
SUB = 8
F32 = jnp.float32
HI = lax.Precision.HIGHEST


def dot(a, b, dims=((1,), (0,))):
    return lax.dot_general(a, b, (dims, ((), ())), precision=HI, preferred_element_type=F32)


def eliminate(block):
    shape = (SUB, BLK)
    groups = [block[g * SUB:(g + 1) * SUB, :] for g in range(BLK // SUB)]
    lane = lax.broadcasted_iota(jnp.int32, shape, 1)
    sub = lax.broadcasted_iota(jnp.int32, shape, 0)
    for g in range(len(groups)):
        base = g * SUB
        rows = groups[g]
        cols = [jnp.broadcast_to(rows[:, base + j:base + j + 1], shape) for j in range(SUB)]
        out = rows
        for s in range(SUB):
            raw = jnp.broadcast_to(rows[s:s + 1, :], shape)
            here = lane == base + s
            mine = sub == s
            out = jnp.where(mine, raw, out)
            inverse = 1.0 / jnp.broadcast_to(cols[s][s:s + 1, :], shape)
            factor = jnp.where(mine, 0.0, cols[s] * inverse)
            unit = jnp.where(here, 1.0, raw)
            kept = jnp.where(here, 0.0, rows)
            rows = jnp.where(mine, unit * inverse, kept - factor * unit)
            for j in range(s + 1, SUB):
                head = jnp.broadcast_to(cols[j][s:s + 1, :], shape)
                cols[j] = jnp.where(mine, head * inverse, cols[j] - factor * head)
        groups[g] = out
        if g + 1 == len(groups):
            break
        reduced = [jnp.broadcast_to(rows[s:s + 1, :], shape) for s in range(SUB)]
        inside = jnp.logical_and(lane >= base, lane < base + SUB)
        for h in range(g + 1, len(groups)):
            old = groups[h]
            terms = [
                jnp.broadcast_to(old[:, base + s:base + s + 1], shape) * reduced[s] for s in range(SUB)
            ]
            while len(terms) > 1:
                terms = [terms[i] + terms[i + 1] for i in range(0, len(terms), 2)]
            groups[h] = jnp.where(inside, 0.0, old) - terms[0]
    return jnp.concatenate(groups, axis=0)


def factor_kernel(a_ref, l_ref, x_ref, w_ref):
    size = a_ref.shape[0]
    count = size // BLK
    row_id = lax.broadcasted_iota(jnp.int32, (BLK, BLK), 0)
    col_id = lax.broadcasted_iota(jnp.int32, (BLK, BLK), 1)

    @pl.loop(0, count)
    def _(i):
        at = pl.ds(pl.multiple_of(i * BLK, BLK), BLK)
        w_ref[at, :] = a_ref[at, :]
        l_ref[at, :] = jnp.zeros((BLK, size), F32)

    @pl.loop(0, count)
    def _(k):
        at = pl.ds(pl.multiple_of(k * BLK, BLK), BLK)
        done = eliminate(w_ref[at, at])
        pivots = jnp.sum(jnp.where(row_id == col_id, done, 0.0), axis=1, keepdims=True)
        scale = 1.0 / jnp.sqrt(pivots)
        upper = jnp.where(col_id >= row_id, done * scale, 0.0)
        inner = jnp.where(col_id < row_id, done * scale, 0.0) + jnp.where(row_id == col_id, scale, 0.0)
        l_ref[at, at] = upper.T
        row = dot(inner, w_ref[at, :])
        block_id = lax.broadcasted_iota(jnp.int32, (BLK, size), 1) // BLK
        row = jnp.where(block_id == k, jnp.concatenate([inner] * count, axis=1), row)
        x_ref[at, :] = jnp.where(block_id <= k, row, 0.0)
        inner_t = inner.T

        @pl.loop(k + 1, count)
        def _(i):
            there = pl.ds(pl.multiple_of(i * BLK, BLK), BLK)
            left = dot(w_ref[there, at], inner_t)
            l_ref[there, at] = left
            w_ref[there, at] = jnp.zeros((BLK, BLK), F32)
            w_ref[there, :] = w_ref[there, :] - dot(left, row)


def factor(a):
    size = a.shape[0]
    shape = jax.ShapeDtypeStruct((size, size), F32)
    return pl.pallas_call(
        factor_kernel,
        out_shape=(shape, shape),
        in_specs=[pl.BlockSpec(memory_space=pltpu.VMEM)],
        out_specs=(pl.BlockSpec(memory_space=pltpu.VMEM),) * 2,
        scratch_shapes=[pltpu.VMEM((size, size), F32)],
        compiler_params=pltpu.CompilerParams(vmem_limit_bytes=32 * 1024 * 1024),
        cost_estimate=pl.CostEstimate(flops=60_000_000_000, bytes_accessed=3 * size * size * 4, transcendentals=0),
        name="factor",
    )(a)


def left_kernel(v_ref, pivot_ref, u_ref, out_ref):
    inner = lax.dot_general(
        v_ref[...], pivot_ref[...], (((0,), (0,)), ((), ())), preferred_element_type=F32
    ).astype(jnp.bfloat16)
    out_ref[...] = jnp.dot(u_ref[...], inner, preferred_element_type=F32).astype(jnp.bfloat16)


def left_factors(v, pivot_v, u):
    slots = v.shape[0] // TILE
    rows = u.shape[0] // slots
    return pl.pallas_call(
        left_kernel,
        grid=(v.shape[1] // RANK, slots),
        out_shape=jax.ShapeDtypeStruct(u.shape, jnp.bfloat16),
        in_specs=[
            pl.BlockSpec((TILE, RANK), lambda j, t: (t, j)),
            pl.BlockSpec((TILE, RANK), lambda j, t: (0, j)),
            pl.BlockSpec((rows, RANK), lambda j, t: (t, j)),
        ],
        out_specs=pl.BlockSpec((rows, RANK), lambda j, t: (t, j)),
        cost_estimate=pl.CostEstimate(
            flops=2 * v.size * RANK + 2 * u.size * RANK,
            bytes_accessed=2 * (v.size + 2 * u.size + pivot_v.size),
            transcendentals=0,
        ),
        name="left",
    )(v, pivot_v, u)


MESH = pl.DeviceIdType.MESH


def exchange_kernel(depth, chips, part_ref, out_ref, got, sends, recvs, pair_send, pair_recv):
    me = lax.axis_index("row")
    col = lax.axis_index("col")
    chip, core = me // 2, me % 2
    share = part_ref.shape[0]
    sub = share // depth
    pair = chip * 2 + 1 - core
    cols = [(col + d) % depth for d in range(1, depth)]
    peers = [((chip + d) % chips) * 2 + core for d in range(1, chips)]

    barrier = pltpu.get_barrier_semaphore()
    for other in cols:
        pl.semaphore_signal(barrier, inc=1, device_id=(me, other), device_id_type=MESH)
    for other in peers + [pair]:
        pl.semaphore_signal(barrier, inc=1, device_id=(other, col), device_id_type=MESH)
    pl.semaphore_wait(barrier, depth + chips - 1)

    def copy(src, dst, i, target):
        return pltpu.make_async_remote_copy(
            src_ref=src, dst_ref=dst, send_sem=sends.at[i], recv_sem=recvs.at[i],
            device_id=target, device_id_type=MESH,
        )

    first = []
    for d, other in enumerate(cols):
        rows = pl.ds(pl.multiple_of(other * sub, sub), sub)
        first.append(copy(part_ref.at[rows, :], got.at[d], d, (me, other)))
        first[-1].start()
    total = part_ref[pl.ds(pl.multiple_of(col * sub, sub), sub), :]
    for d, item in enumerate(first):
        item.wait_recv()
        total = total + got[d]
    mine = pl.ds(pl.multiple_of(me * share + col * sub, sub), sub)
    out_ref[mine, :] = total

    second = []
    for d, other in enumerate(cols):
        second.append(copy(out_ref.at[mine, :], out_ref.at[mine, :], depth - 1 + d, (me, other)))
        second[-1].start()
    for item in second:
        item.wait_recv()

    block = out_ref.at[pl.ds(pl.multiple_of(me * share, share), share), :]
    third = []
    for d, other in enumerate(peers):
        third.append(copy(block, block, 2 * (depth - 1) + d, (other, col)))
        third[-1].start()
    fourth = []
    for d in range(chips):
        if d:
            third[d - 1].wait_recv()
        owner = ((chip + chips - d) % chips) * 2 + core
        held = out_ref.at[pl.ds(pl.multiple_of(owner * share, share), share), :]
        fourth.append(
            pltpu.make_async_remote_copy(
                src_ref=held, dst_ref=held, send_sem=pair_send.at[d], recv_sem=pair_recv.at[d],
                device_id=(pair, col), device_id_type=MESH,
            )
        )
        fourth[-1].start()
    for item in fourth:
        item.wait_recv()
    for item in first + second + third + fourth:
        item.wait_send()


def exchange(mesh, part):
    row_devices, depth = mesh.shape["row"], mesh.shape["col"]
    chips = row_devices // 2
    share, width = part.shape
    links = 2 * (depth - 1) + chips - 1
    return pl.pallas_call(
        functools.partial(exchange_kernel, depth, chips),
        out_shape=jax.ShapeDtypeStruct((share * row_devices, width), F32),
        in_specs=[pl.BlockSpec(memory_space=pltpu.VMEM)],
        out_specs=pl.BlockSpec(memory_space=pltpu.VMEM),
        scratch_shapes=[
            pltpu.VMEM((depth - 1, share // depth, width), F32),
            pltpu.SemaphoreType.DMA((links,)),
            pltpu.SemaphoreType.DMA((links,)),
            pltpu.SemaphoreType.DMA((chips,)),
            pltpu.SemaphoreType.DMA((chips,)),
        ],
        compiler_params=pltpu.CompilerParams(collective_id=0, has_side_effects=True),
        cost_estimate=pl.CostEstimate(flops=40_000_000_000, bytes_accessed=share * row_devices * width * 8, transcendentals=0),
        name="exchange",
    )(part)


def place(block, width, start):
    return lax.dynamic_update_slice_in_dim(jnp.zeros((block.shape[0], width), block.dtype), block, start, 1)


def local(mesh, panel_tiles, left_u, earlier_right_factors, tile_global_index):
    row_devices = mesh.shape["row"]
    tile_count = tile_global_index.shape[0]
    rows, col_width = panel_tiles.shape
    slots = rows // TILE
    pivot_position = jnp.sum(
        jnp.where(tile_global_index == 0, jnp.arange(tile_count, dtype=jnp.int32), 0)
    )
    owner_row = pivot_position // slots
    local_slot = pivot_position % slots
    my_row = lax.axis_index("row")
    my_col = lax.axis_index("col")
    mine = my_row == owner_row

    def owned(value):
        part = lax.dynamic_slice_in_dim(value, local_slot * TILE, TILE, 0)
        return jnp.where(mine, part, jnp.zeros_like(part))

    pivot_right, pivot_left = lax.psum((owned(earlier_right_factors), owned(left_u)), "row")
    pivot_panel, pivot_right, pivot_left = lax.optimization_barrier(
        (owned(panel_tiles), pivot_right, pivot_left)
    )
    pivot_panel = lax.psum_scatter(pivot_panel, "row", scatter_dimension=0, tiled=True)

    share = TILE // row_devices
    my_left = lax.dynamic_slice_in_dim(pivot_left, my_row * share, share, 0)
    pivot_small = left_factors(pivot_right, pivot_right, my_left)
    contract = (((1,), (1,)), ((), ()))
    pivot_terms = lax.dot_general(pivot_small, pivot_left, contract, preferred_element_type=F32)
    diagonal = place(pivot_panel, TILE, my_col * col_width) - pivot_terms

    left_small = left_factors(earlier_right_factors, pivot_right, left_u)
    update_terms = lax.dot_general(left_small, pivot_left, contract, preferred_element_type=F32)
    partial = place(panel_tiles, TILE, my_col * col_width) - update_terms
    partial, diagonal = lax.optimization_barrier((partial, diagonal))
    diagonal = exchange(mesh, diagonal)
    updated = lax.psum_scatter(partial, "col", scatter_dimension=0, tiled=True)

    chol, inverse = factor((diagonal + diagonal.T) * 0.5)
    solved = lax.dot_general(updated, inverse, contract, precision=HI, preferred_element_type=F32)
    held = updated.shape[0]
    first = my_col * held
    chosen = jnp.logical_and(mine, first // TILE == local_slot)
    chol_rows = lax.dynamic_slice_in_dim(chol, first % TILE, held, 0)
    solved = jnp.where(chosen, chol_rows, solved)
    return lax.all_to_all(solved, "col", split_axis=1, concat_axis=0, tiled=True)


def solution(mesh):
    in_specs = (P("row", "col"), P("row", "col"), P("row", "col"), P())
    return jax.shard_map(
        functools.partial(local, mesh), mesh=mesh, in_specs=in_specs, out_specs=P("row", "col"), check_vma=False
    )
```

profile of v0, /device:TPU:0, one launch (start us, length us, event | category | flops | bytes accessed | tf_op | source)
XLA Modules:
  0.0 399.1 jit_solution(16860915745136597625)
XLA Ops:
  6.5 0.0 all-reduce.3.cloned.1.call-start
  6.5 1.3 fusion.1
  10.5 6.6 %dynamic-slice_select_fusion = (bf16[1024,1536]{1,0:T(8,128)(2,1)}, bf16[1024,1536]{1,0:T(8,128)(2,1)}) fusion(bf16[2048,1536]{1,0:T(8,128)(2,1)} %u_ref.1, s32[]{:T(128)S(6)} %select_n.72, pred[]{:T(512)S(6)} %eq.13, bf16[2048,1536]{1,0:T(8,128)(2,1)} %v_ref.1), kind=kLoop, calls=%fused_computation.3 | loop fusion | flops 3145728 | bytes 12582917 | tf_op jit(solution)/shard_map/jit(_where)/select_n | solution.py:254
  17.1 0.0 all-reduce.3.cloned.1.call-update
  17.1 0.0 reduce-scatter.3.cloned.1.call-start
  17.1 1.5 copy-done.2
  18.6 1.0 dynamic-slice_select_fusion.3
  19.7 4.3 %broadcast_in_dim.11 = f32[2048,1024]{1,0:T(8,128)} broadcast(f32[]{:T(128)} %constant.63.clone.1), dimensions={} | broadcast | bytes 8388612 | tf_op jit(solution)/shard_map/broadcast_in_dim | solution.py:235
  24.0 1.5 constant_dynamic-update-slice_fusion.1
  25.5 98.4 %all-reduce.3.cloned.1.call-done = (bf16[1024,1536]{1,0:T(8,128)(2,1)}, bf16[1024,1536]{1,0:T(8,128)(2,1)}) async-done(((bf16[1024,1536]{1,0:T(8,128)(2,1)}, bf16[1024,1536]{1,0:T(8,128)(2,1)}), (bf16[1024,1536]{1,0:T(8,128)(2,1)}, bf16[1024,1536]{1,0:T(8,128)(2,1)})) %all-reduce.3.cloned.1.call-update) | async-done | bytes 6291472 | tf_op jit(solution)/shard_map/psum | solution.py:256
  123.9 0.0 reduce-scatter.3.cloned.1.call-update
  123.9 0.2 reduce-scatter.5.cloned.1.call-start
  124.2 16.3 %left.2 = bf16[2048,1536]{1,0:T(8,128)(2,1)} custom-call(bf16[2048,1536]{1,0:T(8,128)(2,1)} %v_ref.1, bf16[1024,1536]{1,0:T(8,128)(2,1)} %get-tuple-element.12.pivot_ref.v_ref, bf16[2048,1536]{1,0:T(8,128)(2,1)} %u_ref.1), custom_call_target="tpu_custom_call" | custom-call | flops 3221225472 | bytes 22020096 | tf_op jit(solution)/shard_map/left/pallas_call | solution.py:123
  140.4 0.8 constant_dynamic-slice_fusion.u_ref
  141.2 6.7 %left.3 = bf16[128,1536]{1,0:T(8,128)(2,1)} custom-call(bf16[1024,1536]{1,0:T(8,128)(2,1)} %get-tuple-element.12.pivot_ref.v_ref, bf16[1024,1536]{1,0:T(8,128)(2,1)} %get-tuple-element.12.pivot_ref.v_ref, bf16[128,1536]{1,0:T(8,128)(2,1)} %constant_dynamic-slice_fusion.u_ref), custom_call_target="tpu_custom_call" | custom-call | flops 905969664 | bytes 7077888 | tf_op jit(solution)/shard_map/left/pallas_call | solution.py:123
  147.9 13.1 %convolution_subtract_fusion = f32[2048,1024]{1,0:T(8,128)} fusion(f32[2048,1024]{1,0:T(8,128)} %constant_dynamic-update-slice_fusion.1, bf16[2048,1536]{1,0:T(8,128)(2,1)} %left.2, bf16[1024,1536]{1,0:T(8,128)(2,1)S(1)} %copy-done.3), kind=kOutput, calls=%fused_computation.2 | convolution fusion | flops 6444548096 | bytes 26214400 | tf_op jit(solution)/shard_map/dot_general | solution.py:270
  161.0 2.2 reduce-scatter.3.cloned.1.call-done
  163.2 0.9 constant_dynamic-update-slice_fusion
  164.2 1.9 convolution_subtract_fusion.1.part_ref
  166.1 0.0 reduce-scatter.5.cloned.1.call-update
  166.2 68.2 %exchange.1 = f32[1024,1024]{1,0:T(8,128)} custom-call(f32[128,1024]{1,0:T(8,128)} %convolution_subtract_fusion.1.part_ref), custom_call_target="tpu_custom_call" | custom-call | flops 40000000000 | bytes 8388608 | tf_op jit(solution)/shard_map/exchange/pallas_call | solution.py:216
  234.4 5.4 %copy.7 = f32[1024,1024]{0,1:T(8,128)} copy(f32[1024,1024]{1,0:T(8,128)} %exchange.1) | data formatting | bytes 8388608 | tf_op jit(solution)/shard_map/exchange/pallas_call | solution.py:216
  239.7 4.5 %fusion.a_ref = f32[1024,1024]{1,0:T(8,128)S(1)} fusion(f32[1024,1024]{1,0:T(8,128)} %exchange.1, f32[1024,1024]{0,1:T(8,128)} %copy.7), kind=kLoop, calls=%fused_computation.1 | loop fusion | flops 2097152 | bytes 12582912 | tf_op jit(solution)/shard_map/mul | solution.py:276
  244.2 66.3 %factor.1 = (f32[1024,1024]{1,0:T(8,128)S(1)}, f32[1024,1024]{1,0:T(8,128)S(1)}) custom-call(f32[1024,1024]{1,0:T(8,128)S(1)} %fusion.a_ref), custom_call_target="tpu_custom_call" | custom-call | flops 60000002048 | bytes 12582912 | tf_op jit(solution)/shard_map/factor/pallas_call | solution.py:101
  310.6 0.0 copy-start
  310.6 1.9 copy-done
  312.5 2.0 copy-done.1
  314.5 9.8 %reduce-scatter.5.cloned.1.call-done = f32[512,1024]{1,0:T(8,128)} async-done(((f32[2048,1024]{1,0:T(8,128)}), f32[512,1024]{1,0:T(8,128)}) %reduce-scatter.5.cloned.1.call-update) | async-done | bytes 2097168 | tf_op jit(solution)/shard_map/reduce_scatter | solution.py:274
  324.3 10.2 %dynamic-slice_select_fusion.2 = f32[512,1024]{1,0:T(8,128)S(1)} fusion(f32[1024,1024]{1,0:T(8,128)} %copy-done.1, s32[]{:T(128)S(6)} %select_n.79, f32[512,1024]{1,0:T(8,128)} %reduce-scatter.5.cloned.1.call-done, f32[1024,1024]{1,0:T(8,128)} %copy-done, pred[]{:T(512)S(6)} %and.26), kind=kOutput, calls=%fused_computation.6 | convolution fusion | flops 6442975232 | bytes 10485765 | tf_op jit(solution)/shard_map/dot_general | solution.py:277
  334.4 0.2 copy.11
  334.6 56.6 %all_to_all.19 = f32[512,4,256]{2,0,1:T(8,128)S(1)} all-to-all(f32[512,4,256]{2,0,1:T(8,128)S(1)} %bitcast.17), channel_id=1, replica_groups=mesh['row'=8,'col'=4] {'col'}, dimensions={1} | all-to-all | bytes 4194304 | tf_op jit(solution)/shard_map/all_to_all | solution.py:283
  391.2 1.3 copy.17
  (7 shorter events, 0.1 us)
Async XLA Ops:
  6.5 117.4 %all-reduce.3.cloned.1.call-start = ((), (), s32[]{:S(2)}) async-start(), calls=%async_computation.5 | async-start | bytes 12582912 | tf_op jit(solution)/shard_map/psum | solution.py:256
  17.1 1.6 copy-start.2
  17.1 146.1 %reduce-scatter.3.cloned.1.call-start = ((), (), s32[]{:S(2)}) async-start(), calls=%async_computation.3 | async-start | bytes 1179648 | tf_op jit(solution)/shard_map/reduce_scatter | solution.py:260
  123.9 16.5 %copy-start.3 = (bf16[1024,1536]{1,0:T(8,128)(2,1)S(1)}, bf16[1024,1536]{1,0:T(8,128)(2,1)}, u32[]{:S(2)}) copy-start(bf16[1024,1536]{1,0:T(8,128)(2,1)} %get-tuple-element.13) | copy-start | bytes 9437188
  123.9 200.3 %reduce-scatter.5.cloned.1.call-start = ((), (), s32[]{:S(2)}) async-start(), calls=%async_computation.4 | async-start | bytes 10485760 | tf_op jit(solution)/shard_map/reduce_scatter | solution.py:274
  147.9 16.3 %copy-start.4 = (bf16[128,1536]{1,0:T(8,128)(2,1)S(1)}, bf16[128,1536]{1,0:T(8,128)(2,1)}, u32[]{:S(2)}) copy-start(bf16[128,1536]{1,0:T(8,128)(2,1)} %left.3) | copy-start | bytes 1179652
  310.6 1.9 copy-start
  312.5 2.0 copy-start.1
Sparse Core Ops, SparseCore 0:
  17.2 106.6 all-reduce.2
  127.1 36.0 reduce-scatter.2
  166.2 157.9 reduce-scatter.4
where the time goes:
time: 400 us; the launch traced here: 399 us
  Pallas kernels  157 us (39%)
  waiting for transfers between devices  110 us (28%)
  blocking collectives  56.6 us (14%)
  matrix products  25.2 us (6%)
  local copies, waits for them, and re-layouts  19.8 us (5%)
  between operations  15.9 us (4%)
  other arithmetic  13.4 us (3%)
    psum x1, waiting for transfers between devices, local(): lax.psum((owned(earlier_right_factors), owned(left_u)), 'row')  98.4 us
    pallas_call x1, Pallas kernels, exchange(): pl.pallas_call(functools.partial(exchange_kernel, depth, chips), out_shap...  68.2 us
    pallas_call x1, Pallas kernels, factor(): pl.pallas_call(factor_kernel, out_shape=(shape, shape), in_specs=[pl.Bloc...  66.3 us
    all_to_all x1, blocking collectives, local(): lax.all_to_all(solved, 'col', split_axis=1, concat_axis=0, tiled=True)  56.6 us
    pallas_call x2, Pallas kernels, left_factors(): pl.pallas_call(left_kernel, grid=(v.shape[1] // RANK, slots), out_shape=j...  23 us
    dot_general x1, matrix products, local(): lax.dot_general(left_small, pivot_left, contract, preferred_element_type=...  13.1 us
    dot_general x1, matrix products, local(): lax.dot_general(updated, inverse, contract, precision=HI, preferred_eleme...  10.2 us
    reduce_scatter x1, waiting for transfers between devices, local(): updated = lax.psum_scatter(partial, 'col', scatter_dimension=0, tiled=True)  9.79 us
  transfers between devices with their start and end apart: 3, of which 3 were waited for; matrix products, arithmetic and copies ran while one was open for 8% of the time, Pallas kernels for 39%

commit v1 on v0

v1 whole, which is shorter than its diff:
```python
import functools

import jax
import jax.numpy as jnp
from jax import lax
from jax.experimental import pallas as pl
from jax.experimental.pallas import tpu as pltpu
from jax.sharding import PartitionSpec as P

TILE = 1024
RANK = 256

BLK = 128
SUB = 8
F32 = jnp.float32
BF16 = jnp.bfloat16
HI = lax.Precision.HIGHEST
MESH = pl.DeviceIdType.MESH
ANY = pl.BlockSpec(memory_space=pl.ANY)
VM = pl.BlockSpec(memory_space=pltpu.VMEM)
TRANS = (((1,), (1,)), ((), ()))


def dot(a, b, dims=((1,), (0,))):
    return lax.dot_general(a, b, (dims, ((), ())), precision=HI, preferred_element_type=F32)


def window(start, size):
    return pl.ds(pl.multiple_of(start, size), size)


def remote(src, dst, send, recv, target):
    return pltpu.make_async_remote_copy(
        src_ref=src, dst_ref=dst, send_sem=send, recv_sem=recv, device_id=target, device_id_type=MESH
    )


def pick(table, index):
    value = jnp.int32(table[0])
    for i in range(1, len(table)):
        value = jnp.where(index == i, jnp.int32(table[i]), value)
    return value


def spread_kernel(
    owner, row_devices, pieces, v_mine, u_mine, a_mine, v_ref, u_ref, left_ref, pu_ref, part_ref,
    pv, v_own, u_own, pvt, a_got, sends, recvs, a_send, a_recv, local_sem,
):
    me = lax.axis_index("row")
    col = lax.axis_index("col")
    chips = row_devices // 2
    chip, core = me // 2, me % 2
    order = [i ^ (i >> 1) for i in range(chips)]
    if len(set(order)) != chips or max(order) >= chips:
        order = list(range(chips))
    place_of = [order.index(c) for c in range(chips)]
    home = place_of[owner // 2]
    place = pick(place_of, chip)
    forward = 1 - 2 * core
    hops = (chips + forward * (place - home)) % chips
    onward = pick(order, (place + chips + forward) % chips) * 2 + core
    pair = chip * 2 + 1 - core
    tile, width = pu_ref.shape
    half = tile // 2
    step = half // pieces
    share = tile // row_devices
    rank = RANK
    blocks = width // rank
    slots = v_ref.shape[0] // tile

    loads = [
        pltpu.make_async_copy(v_ref, v_own, local_sem.at[0]),
        pltpu.make_async_copy(u_ref, u_own, local_sem.at[1]),
    ]
    for item in loads:
        item.start()

    barrier = pltpu.get_barrier_semaphore()
    for d in range(1, row_devices):
        pl.semaphore_signal(barrier, inc=1, device_id=((me + d) % row_devices, col), device_id_type=MESH)
    pl.semaphore_wait(barrier, row_devices - 1)

    def rows(stream, i):
        return window(stream * half + i * step, step)

    def hop(kind, stream, i, target, src=None):
        dst = (pv, pu_ref)[kind].at[rows(stream, i), :]
        return remote(
            dst if src is None else src.at[rows(stream, i), :], dst,
            sends.at[kind, stream, i], recvs.at[kind, stream, i], target,
        )

    def cross(kind, stream, i, target, src=None):
        dst = (pv, pu_ref)[kind].at[rows(stream, i), :]
        return remote(
            dst if src is None else src.at[rows(stream, i), :], dst,
            sends.at[2 + kind, stream, i], recvs.at[kind, stream, i], target,
        )

    is_owner = me == owner
    away = chip != owner // 2
    last = hops == chips - 1
    to_right = order[(home + 1) % chips] * 2
    to_left = order[(home + chips - 1) % chips] * 2 + 1
    mine = [v_mine, u_mine]
    own_copy = [
        pltpu.make_async_copy(v_mine, pv, local_sem.at[2]),
        pltpu.make_async_copy(u_mine, pu_ref, local_sem.at[3]),
        pltpu.make_async_copy(a_mine.at[window(owner * share, share), :], a_got, local_sem.at[4]),
    ]

    def a_piece(target):
        return remote(a_mine.at[window(target * share, share), :], a_got, a_send.at[target], a_recv, (target, col))

    @pl.when(is_owner)
    def _():
        for kind in range(2):

            @pl.loop(0, pieces)
            def _(i):
                hop(kind, 0, i, (to_right, col), mine[kind]).start()
                hop(kind, 1, i, (to_left, col), mine[kind]).start()
                cross(kind, 0, i, (pair, col), mine[kind]).start()
                cross(kind, 1, i, (pair, col), mine[kind]).start()

            if kind == 0:
                for other in range(row_devices):
                    if other != owner:
                        a_piece(other).start()
        for item in own_copy:
            item.start()

    def relay(kind, i):
        @pl.when(away)
        def _():
            hop(kind, core, i, (onward, col)).wait_recv()

            @pl.when(jnp.logical_not(last))
            def _():
                hop(kind, core, i, (onward, col)).start()

            cross(kind, core, i, (pair, col)).start()

    def gather(kind):
        @pl.when(jnp.logical_not(is_owner))
        def _():
            @pl.loop(0, pieces)
            def _(i):
                cross(kind, 1 - core, i, (pair, col)).wait_recv()

            @pl.when(jnp.logical_not(away))
            def _():
                @pl.loop(0, pieces)
                def _(i):
                    cross(kind, core, i, (pair, col)).wait_recv()

    @pl.loop(0, pieces)
    def _(i):
        relay(0, i)

    gather(0)

    @pl.when(is_owner)
    def _():
        own_copy[0].wait()

    for item in loads:
        item.wait()

    total = blocks * slots
    for b in range(blocks):
        at = slice(b * rank, (b + 1) * rank)
        pvt[at, :] = pv[:, at].T
        for t in range(slots):
            here = slice(t * tile, (t + 1) * tile)
            inner = jnp.dot(pvt[at, :], v_own[here, at], preferred_element_type=F32).astype(BF16)
            left_ref[here, at] = lax.dot_general(
                u_own[here, at], inner, TRANS, preferred_element_type=F32
            ).astype(BF16)
            done = b * slots + t
            for i in range(done * pieces // total, (done + 1) * pieces // total):
                relay(1, i)

    gather(1)

    @pl.when(is_owner)
    def _():
        own_copy[1].wait()
        own_copy[2].wait()

    @pl.when(jnp.logical_not(is_owner))
    def _():
        a_piece(owner).wait_recv()

    small = []
    for b in range(blocks):
        at = slice(b * rank, (b + 1) * rank)
        inner = jnp.dot(pvt[at, :], pv[:, at], preferred_element_type=F32).astype(BF16)
        small.append(
            lax.dot_general(
                pu_ref[window(me * share, share), at], inner, TRANS, preferred_element_type=F32
            ).astype(BF16)
        )
    small = jnp.concatenate(small, axis=1)
    part_ref[...] = -lax.dot_general(small, pu_ref[...], TRANS, preferred_element_type=F32)
    width_out = a_got.shape[1]
    mine_cols = window(col * width_out, width_out)
    part_ref[:, mine_cols] = part_ref[:, mine_cols] + a_got[...]

    @pl.when(is_owner)
    def _():
        for kind in range(2):

            @pl.loop(0, pieces)
            def _(i):
                hop(kind, 0, i, (to_right, col), mine[kind]).wait_send()
                hop(kind, 1, i, (to_left, col), mine[kind]).wait_send()
                cross(kind, 0, i, (pair, col), mine[kind]).wait_send()
                cross(kind, 1, i, (pair, col), mine[kind]).wait_send()

        for other in range(row_devices):
            if other != owner:
                a_piece(other).wait_send()

    @pl.when(away)
    def _():
        for kind in range(2):

            @pl.loop(0, pieces)
            def _(i):
                @pl.when(jnp.logical_not(last))
                def _():
                    hop(kind, core, i, (onward, col)).wait_send()

                cross(kind, core, i, (pair, col)).wait_send()


def spread(mesh, owner, v_mine, u_mine, a_mine, v, u):
    row_devices = mesh.shape["row"]
    tile, width = v_mine.shape
    pieces = 8
    share = tile // row_devices
    return pl.pallas_call(
        functools.partial(spread_kernel, owner, row_devices, pieces),
        out_shape=(
            jax.ShapeDtypeStruct(u.shape, BF16),
            jax.ShapeDtypeStruct((tile, width), BF16),
            jax.ShapeDtypeStruct((share, tile), F32),
        ),
        in_specs=[VM, VM, VM, ANY, ANY],
        out_specs=(VM, VM, VM),
        scratch_shapes=[
            pltpu.VMEM((tile, width), BF16),
            pltpu.VMEM(v.shape, BF16),
            pltpu.VMEM(u.shape, BF16),
            pltpu.VMEM((width, tile), BF16),
            pltpu.VMEM((share, a_mine.shape[1]), F32),
            pltpu.SemaphoreType.DMA((4, 2, pieces)),
            pltpu.SemaphoreType.DMA((2, 2, pieces)),
            pltpu.SemaphoreType.DMA((row_devices,)),
            pltpu.SemaphoreType.DMA,
            pltpu.SemaphoreType.DMA((5,)),
        ],
        compiler_params=pltpu.CompilerParams(
            collective_id=1 + owner, has_side_effects=True, vmem_limit_bytes=48 * 1024 * 1024
        ),
        cost_estimate=pl.CostEstimate(flops=20_000_000_000, bytes_accessed=30_000_000, transcendentals=0),
        name="spread",
    )(v_mine, u_mine, a_mine, v, u)


def eliminate(block):
    shape = (SUB, BLK)
    groups = [block[g * SUB:(g + 1) * SUB, :] for g in range(BLK // SUB)]
    lane = lax.broadcasted_iota(jnp.int32, shape, 1)
    sub = lax.broadcasted_iota(jnp.int32, shape, 0)
    for g in range(len(groups)):
        base = g * SUB
        rows = groups[g]
        cols = [jnp.broadcast_to(rows[:, base + j:base + j + 1], shape) for j in range(SUB)]
        out = rows
        for s in range(SUB):
            raw = jnp.broadcast_to(rows[s:s + 1, :], shape)
            here = lane == base + s
            mine = sub == s
            out = jnp.where(mine, raw, out)
            inverse = 1.0 / jnp.broadcast_to(cols[s][s:s + 1, :], shape)
            factor = jnp.where(mine, 0.0, cols[s] * inverse)
            unit = jnp.where(here, 1.0, raw)
            kept = jnp.where(here, 0.0, rows)
            rows = jnp.where(mine, unit * inverse, kept - factor * unit)
            for j in range(s + 1, SUB):
                head = jnp.broadcast_to(cols[j][s:s + 1, :], shape)
                cols[j] = jnp.where(mine, head * inverse, cols[j] - factor * head)
        groups[g] = out
        if g + 1 == len(groups):
            break
        reduced = [jnp.broadcast_to(rows[s:s + 1, :], shape) for s in range(SUB)]
        inside = jnp.logical_and(lane >= base, lane < base + SUB)
        for h in range(g + 1, len(groups)):
            old = groups[h]
            terms = [
                jnp.broadcast_to(old[:, base + s:base + s + 1], shape) * reduced[s] for s in range(SUB)
            ]
            while len(terms) > 1:
                terms = [terms[i] + terms[i + 1] for i in range(0, len(terms), 2)]
            groups[h] = jnp.where(inside, 0.0, old) - terms[0]
    return jnp.concatenate(groups, axis=0)


def factor_step(k, w_ref, l_ref, x_ref):
    size = w_ref.shape[0]
    count = size // BLK
    row_id = lax.broadcasted_iota(jnp.int32, (BLK, BLK), 0)
    col_id = lax.broadcasted_iota(jnp.int32, (BLK, BLK), 1)
    at = window(k * BLK, BLK)
    done = eliminate(w_ref[at, at])
    pivots = jnp.sum(jnp.where(row_id == col_id, done, 0.0), axis=1, keepdims=True)
    scale = 1.0 / jnp.sqrt(pivots)
    upper = jnp.where(col_id >= row_id, done * scale, 0.0)
    inner = jnp.where(col_id < row_id, done * scale, 0.0) + jnp.where(row_id == col_id, scale, 0.0)
    l_ref[at, at] = upper.T
    row = dot(inner, w_ref[at, :])
    block_id = lax.broadcasted_iota(jnp.int32, (BLK, size), 1) // BLK
    row = jnp.where(block_id == k, jnp.concatenate([inner] * count, axis=1), row)
    x_ref[at, :] = jnp.where(block_id <= k, row, 0.0)
    inner_t = inner.T

    @pl.loop(k + 1, count)
    def _(i):
        there = window(i * BLK, BLK)
        left = dot(w_ref[there, at], inner_t)
        l_ref[there, at] = left
        w_ref[there, at] = jnp.zeros((BLK, BLK), F32)
        w_ref[there, :] = w_ref[there, :] - dot(left, row)


def panel_kernel(
    depth, row_devices, pieces, chunks, part_ref, left_ref, u_ref, a_ref, out_ref, lcol_ref,
    w_ref, l_ref, x_ref, acc, come, got,
    sends, recvs, pair_send, pair_recv, line_send, line_recv, out_send, out_recv,
):
    me = lax.axis_index("row")
    col = lax.axis_index("col")
    chips = row_devices // 2
    chip, core = me // 2, me % 2
    share = part_ref.shape[0]
    sub = share // depth
    pair = chip * 2 + 1 - core
    cols = [(col + d) % depth for d in range(1, depth)]
    peers = [((chip + d) % chips) * 2 + core for d in range(1, chips)]
    size = w_ref.shape[0]
    width = a_ref.shape[1]
    half = acc.shape[0] // 2
    piece = half // pieces
    count = size // BLK

    barrier = pltpu.get_barrier_semaphore()
    for other in cols:
        pl.semaphore_signal(barrier, inc=1, device_id=(me, other), device_id_type=MESH)
    for other in peers + [pair]:
        pl.semaphore_signal(barrier, inc=1, device_id=(other, col), device_id_type=MESH)
    pl.semaphore_wait(barrier, depth + chips - 1)

    first = []
    for d, other in enumerate(cols):
        first.append(
            remote(part_ref.at[window(other * sub, sub), :], got.at[d], sends.at[d], recvs.at[d], (me, other))
        )
        first[-1].start()

    mine_cols = window(col * width, width)

    def fill(lo, hi):
        @pl.loop(lo, hi)
        def _(i):
            at = window(i * 256, 256)
            acc[at, :] = -lax.dot_general(left_ref[at, :], u_ref[...], TRANS, preferred_element_type=F32)
            acc[at, mine_cols] = acc[at, mine_cols] + a_ref[at, :]

    strips = acc.shape[0] // 256
    fill(0, strips // 4)

    total = part_ref[window(col * sub, sub), :]
    for d, item in enumerate(first):
        item.wait_recv()
        total = total + got[d]
    mine = window(me * share + col * sub, sub)
    w_ref[mine, :] = total

    second = []
    for d, other in enumerate(cols):
        n = depth - 1 + d
        second.append(remote(w_ref.at[mine, :], w_ref.at[mine, :], sends.at[n], recvs.at[n], (me, other)))
        second[-1].start()
    fill(strips // 4, strips // 2)
    for item in second:
        item.wait_recv()

    block = w_ref.at[window(me * share, share), :]
    third = []
    for d, other in enumerate(peers):
        n = 2 * (depth - 1) + d
        third.append(remote(block, block, sends.at[n], recvs.at[n], (other, col)))
        third[-1].start()
    fill(strips // 2, strips)
    fourth = []
    for d in range(chips):
        if d:
            third[d - 1].wait_recv()
        holder = ((chip + chips - d) % chips) * 2 + core
        held = w_ref.at[window(holder * share, share), :]
        fourth.append(remote(held, held, pair_send.at[d], pair_recv.at[d], (pair, col)))
        fourth[-1].start()

    def line(way, i, target):
        at = window(way * half + i * piece, piece)
        return remote(acc.at[at, :], come.at[at, :], line_send.at[way, i], line_recv.at[way, i], (me, target))

    def pass_on(way, i, seat, target):
        @pl.when(jnp.logical_and(i >= 0, i < pieces))
        def _():
            at = window(way * half + i * piece, piece)

            @pl.when(seat > 0)
            def _():
                line(way, i, target).wait_recv()
                acc[at, :] = acc[at, :] + come[at, :]

            @pl.when(seat < depth - 1)
            def _():
                line(way, i, target).start()

    up = jnp.minimum(col + 1, depth - 1)
    down = jnp.maximum(col - 1, 0)
    seat_down = depth - 1 - col

    def line_step(tick):
        pass_on(0, tick - seat_down, seat_down, down)
        pass_on(1, tick - col, col, up)

    line_step(0)
    for item in fourth:
        item.wait_recv()
    for item in first + second + third + fourth:
        item.wait_send()

    @pl.loop(0, count)
    def _(i):
        at = window(i * BLK, BLK)
        l_ref[at, :] = jnp.zeros((BLK, size), F32)
        w_ref[at, at] = (w_ref[at, at] + w_ref[at, at].T) * 0.5

        @pl.loop(i + 1, count)
        def _(j):
            there = window(j * BLK, BLK)
            even = (w_ref[at, there] + w_ref[there, at].T) * 0.5
            w_ref[at, there] = even
            w_ref[there, at] = even.T

    ticks = pieces + depth - 1
    per = max(1, (ticks - 1) // count)

    @pl.loop(0, count)
    def _(k):
        @pl.loop(0, per)
        def _(s):
            line_step(1 + k * per + s)

        factor_step(k, w_ref, l_ref, x_ref)

    @pl.loop(1 + count * per, ticks)
    def _(tick):
        line_step(tick)

    lcol_ref[...] = l_ref[:, mine_cols]

    chunk = half // chunks

    def deal(way, i, c):
        at = window(way * half + i * chunk, chunk)
        return remote(
            come.at[at, c * width:(c + 1) * width], out_ref.at[at, :],
            out_send.at[i, c], out_recv.at[way, i], (me, c),
        )

    ends = [(0, 0), (1, depth - 1)]
    for way, end in ends:

        @pl.when(col == end)
        def _():
            @pl.loop(0, chunks)
            def _(i):
                at = window(way * half + i * chunk, chunk)
                for c in sorted(range(depth), key=lambda c: -abs(c - end)):
                    upto = (c + 1) * width
                    value = dot(acc[at, :upto], x_ref[c * width:upto, :upto], ((1,), (1,)))
                    if c == end:
                        out_ref[at, :] = value
                    else:
                        come[at, c * width:upto] = value
                        deal(way, i, c).start()

    for way, end in ends:

        @pl.when(col != end)
        def _():
            @pl.loop(0, chunks)
            def _(i):
                deal(way, i, 0).wait_recv()

    for way, end in ends:

        @pl.when(col == end)
        def _():
            @pl.loop(0, chunks)
            def _(i):
                for c in range(depth):
                    if c != end:
                        deal(way, i, c).wait_send()

    @pl.when(col > 0)
    def _():
        @pl.loop(0, pieces)
        def _(i):
            line(0, i, down).wait_send()

    @pl.when(col < depth - 1)
    def _():
        @pl.loop(0, pieces)
        def _(i):
            line(1, i, up).wait_send()


def panel(mesh, part, left, pivot_u, tiles):
    row_devices, depth = mesh.shape["row"], mesh.shape["col"]
    chips = row_devices // 2
    share, size = part.shape
    rows, width = tiles.shape
    pieces = rows // 2 // 64
    chunks = rows // 2 // 128
    links = 2 * (depth - 1) + chips - 1
    return pl.pallas_call(
        functools.partial(panel_kernel, depth, row_devices, pieces, chunks),
        out_shape=(
            jax.ShapeDtypeStruct((rows, width), F32),
            jax.ShapeDtypeStruct((size, width), F32),
        ),
        in_specs=[VM] * 4,
        out_specs=(VM, VM),
        scratch_shapes=[
            pltpu.VMEM((size, size), F32),
            pltpu.VMEM((size, size), F32),
            pltpu.VMEM((size, size), F32),
            pltpu.VMEM((rows, size), F32),
            pltpu.VMEM((rows, size), F32),
            pltpu.VMEM((depth - 1, share // depth, size), F32),
            pltpu.SemaphoreType.DMA((links,)),
            pltpu.SemaphoreType.DMA((links,)),
            pltpu.SemaphoreType.DMA((chips,)),
            pltpu.SemaphoreType.DMA((chips,)),
            pltpu.SemaphoreType.DMA((2, pieces)),
            pltpu.SemaphoreType.DMA((2, pieces)),
            pltpu.SemaphoreType.DMA((chunks, depth)),
            pltpu.SemaphoreType.DMA((2, chunks)),
        ],
        compiler_params=pltpu.CompilerParams(
            collective_id=0, has_side_effects=True, vmem_limit_bytes=58 * 1024 * 1024
        ),
        cost_estimate=pl.CostEstimate(flops=60_000_000_000, bytes_accessed=30_000_000, transcendentals=0),
        name="panel",
    )(part, left, pivot_u, tiles)


def local(mesh, panel_tiles, left_u, earlier_right_factors, tile_global_index):
    row_devices = mesh.shape["row"]
    tile_count = tile_global_index.shape[0]
    slots = panel_tiles.shape[0] // TILE
    pivot_position = jnp.sum(
        jnp.where(tile_global_index == 0, jnp.arange(tile_count, dtype=jnp.int32), 0)
    )
    owner_row = pivot_position // slots
    local_slot = pivot_position % slots

    def slot(value):
        return lax.dynamic_slice_in_dim(value, local_slot * TILE, TILE, 0)

    branches = [functools.partial(spread, mesh, owner) for owner in range(row_devices)]
    left, pivot_u, part = lax.switch(
        owner_row, branches,
        slot(earlier_right_factors), slot(left_u), slot(panel_tiles), earlier_right_factors, left_u,
    )
    solved, chol = panel(mesh, part, left, pivot_u, panel_tiles)
    chosen = jnp.logical_and(lax.axis_index("row") == owner_row, jnp.arange(slots) == local_slot)
    solved = solved.reshape(slots, TILE, -1)
    return jnp.where(chosen[:, None, None], chol[None], solved).reshape(panel_tiles.shape)


def solution(mesh):
    in_specs = (P("row", "col"), P("row", "col"), P("row", "col"), P())
    return jax.shard_map(
        functools.partial(local, mesh), mesh=mesh, in_specs=in_specs, out_specs=P("row", "col"), check_vma=False
    )
```

time: 400 us -> 377 us (0.943)
  Pallas kernels: 157 us -> 332 us
  waiting for transfers between devices: 110 us -> 0 us
  blocking collectives: 56.6 us -> 0 us
  loops' own time: 0 us -> 31.8 us
  matrix products: 25.2 us -> 0 us
  local copies, waits for them, and re-layouts: 19.8 us -> 6.23 us
  between operations: 15.9 us -> 3.03 us
  other arithmetic: 13.4 us -> 4.84 us
    pallas_call x4 -> x2, Pallas kernels: 157 us -> 332 us  [the longest x1 280 us: panel(): pl.pallas_call(functools.partial(panel_kernel, depth, row_devices, pieces...]
    psum x1 -> x0, waiting for transfers between devices: 98.4 us -> none  [local(): lax.psum((owned(earlier_right_factors), owned(left_u)), 'row')]
    all_to_all x1 -> x0, blocking collectives: 56.6 us -> none  [local(): lax.all_to_all(solved, 'col', split_axis=1, concat_axis=0, tiled=True)]
    another operation x0 -> x1, loops' own time: none -> 31.8 us  [local(): lax.switch(owner_row, branches, slot(earlier_right_factors), slot(left_u)...]
    dot_general x3 -> x0, matrix products: 25.2 us -> none  [the longest x1 13.1 us: local(): lax.dot_general(left_small, pivot_left, contract, preferred_element_type=...]
    reduce_scatter x2 -> x0, waiting for transfers between devices: 12 us -> none  [the longest x1 9.79 us: local(): updated = lax.psum_scatter(partial, 'col', scatter_dimension=0, tiled=True)]
    unnamed x11 -> x2, local copies, waits for them, and re-layouts: 6.74 us -> 0.01 us
    dynamic_slice x1 -> x2, local copies, waits for them, and re-layouts: 0.76 us -> 6.13 us  [slot(): return lax.dynamic_slice_in_dim(value, local_slot * TILE, TILE, 0)]
  transfers between devices with their start and end apart: 3 -> 0, of which waited for: 3 -> 0; matrix products, arithmetic and copies ran while one was open for 8% -> 0% of each run, Pallas kernels for 39% -> 0%
where the time goes in v1:
time: 377 us
  Pallas kernels  332 us (88%)
  loops' own time  31.8 us (8%)
  local copies, waits for them, and re-layouts  6.23 us (2%)
  other arithmetic  4.84 us (1%)
    pallas_call x1, Pallas kernels, panel(): pl.pallas_call(functools.partial(panel_kernel, depth, row_devices, pieces...  280 us
    pallas_call x1, Pallas kernels, spread(): pl.pallas_call(functools.partial(spread_kernel, owner, row_devices, piece...  51.3 us
    another operation x1, loops' own time, local(): lax.switch(owner_row, branches, slot(earlier_right_factors), slot(left_u)...  31.8 us

profile of v1, /device:TPU:0, one launch (start us, length us, event | category | flops | bytes accessed | tf_op | source)
XLA Modules:
  0.0 377.4 jit_solution(3892337657718385567)
XLA Ops:
  0.0 1.3 fusion
  3.2 0.0 copy-start
  3.2 5.1 %constant_dynamic-slice_fusion.1 = (bf16[1024,1536]{1,0:T(8,128)(2,1)S(1)}, bf16[1024,1536]{1,0:T(8,128)(2,1)}) fusion(bf16[2048,1536]{1,0:T(8,128)(2,1)} %param.13, s32[]{:T(128)S(6)} %select_n.28, bf16[2048,1536]{1,0:T(8,128)(2,1)} %param.14), kind=kLoop, calls=%fused_computation.4 | loop fusion | bytes 12582916 | tf_op jit(solution)/shard_map/dynamic_slice | solution.py:586
  8.3 0.0 copy-done
  8.3 1.0 constant_dynamic-slice_fusion
  10.0 83.1 %conditional.1 = ((bf16[2048,1536]{1,0:T(8,128)(2,1)}, bf16[1024,1536]{1,0:T(8,128)(2,1)}, f32[128,1024]{1,0:T(8,128)})) conditional(s32[]{:T(128)} %clamp.3, (bf16[1024,1536]{1,0:T(8,128)(2,1)}, bf16[1024,1536]{1,0:T(8,128)(2,1)S(1)}, f32[1024,256]{1,0:T(8,128)}, bf16[2048,1536]{1,0:T(8,128)(2,1)}, ...), branch_computations={%region_1.2_spmd, %region_2.3_spmd, %region_3.4_spmd, %region_4.5_... | conditional | flops 20000000000 | bytes 30000008 | solution.py:589
  10.0 51.3 %spread.8 = (bf16[2048,1536]{1,0:T(8,128)(2,1)}, bf16[1024,1536]{1,0:T(8,128)(2,1)}, f32[128,1024]{1,0:T(8,128)}) custom-call(bf16[1024,1536]{1,0:T(8,128)(2,1)} %get-tuple-element.85.v_mine, bf16[1024,1536]{1,0:T(8,128)(2,1)S(1)} %get-tuple-element.86.u_mine, f32[1024,256]{1,0:T(8,128)} %get-tuple-element.87.a_mine, ...), custom_call_target="tpu_custom_call" | custom-call | flops 20000000000 | bytes 30000000 | tf_op jit(solution)/shard_map/cond/branch_0_fun/spread/pallas_call | solution.py:243
  93.1 280.2 %panel.1 = (f32[2048,256]{1,0:T(8,128)}, f32[1024,256]{1,0:T(8,128)}) custom-call(f32[128,1024]{1,0:T(8,128)} %get-tuple-element.130.part_ref, bf16[2048,1536]{1,0:T(8,128)(2,1)} %get-tuple-element.131.left_ref, bf16[1024,1536]{1,0:T(8,128)(2,1)} %get-tuple-element.132.u_ref, f32[2048,256]{1,0:T(8,128)} %a_ref.1), custom_call_target="tpu_custom_call" | custom-call | flops 60000002048 | bytes 30000000 | tf_op jit(solution)/shard_map/panel/pallas_call | solution.py:543
  373.3 0.1 broadcast_in_dim.26
  373.4 3.5 bitcast_select_fusion
  (2 shorter events, 0.0 us)
Async XLA Ops:
  3.2 5.1 %copy-start = (f32[2048,256]{1,0:T(8,128)S(1)}, f32[2048,256]{1,0:T(8,128)}, u32[]{:S(2)}) copy-start(f32[2048,256]{1,0:T(8,128)} %a_ref.1) | copy-start | bytes 6291460
